TPU v7x, 256 devices: a whole 4x4x8 slice. The times are simulated.
256 devices in a mesh: dp: 4 (over y), tensor: 64 (over x, z, core).
Axes of the slice: x: 4, y: 4, z: 8, core: 2. Of those that a mesh axis runs over, the one named last changes fastest.
Arguments:
- tokens: bfloat16 [4, 8192, 1536], P('dp', 'tensor'), may hold values from -6 to 6
- attn_gain: float32 [1536], replicated, may hold values from 0.1 to 1.9
- qkv_weight: bfloat16 [1536, 2560], P(None, 'dp'), may hold values from -0.25 to 0.25
- out_weight: bfloat16 [1536, 1536], P('dp'), may hold values from -0.15625 to 0.15625
- prefix_cache: bfloat16 [4, 512, 2, 512], P('dp', 'tensor'), may hold values from -640 to 640
- lengths: int32 [4, 256], P('dp'), may hold values from 1 to 384, 8192 in all within a row
- ffn_gain: float32 [1536], replicated, may hold values from 0.1 to 1.9
- expert_ids: int32 [4, 8192, 8], P('dp', 'tensor'), may hold values from 0 to 31, all different within a row; in each aligned block of 128 rows (0 to 127, 128 to 255, ..., all dimensions but the last counted through in order) at most 40 rows name the same one
- gate_weights: float32 [4, 8192, 8], P('dp', 'tensor'), may hold values from 0.05 to 0.5
- expert_in: bfloat16 [64, 1536, 512], P('tensor'), may hold values from -0.15625 to 0.15625
- expert_out: bfloat16 [64, 256, 1536], P('tensor'), may hold values from -0.25 to 0.25
Outputs:
- hidden_state: bfloat16 [4, 8192, 1536], P('dp', 'tensor')
- mixed: bfloat16 [4, 8192, 1536], P('dp', 'tensor')
Inputs may be any that keep to these rules, and one draw needn't show every extreme that they name: `lengths`: each group's 256 requests fill its 8192 suffix positions in order, and the longest holds exactly 384 tokens. `expert_ids`: each token names 8 different experts; among the 128 tokens of one device no expert is named more than 40 times, a bound that some block reaches.
All inputs are finite; a program needn't handle non-finite values.
Results may differ from a plain program's by a relative error of at most 0.014.
The roundings to bfloat16 on the way count: a program that leaves them out, or rounds other values in their place, can miss the bound.
Values may be sent and summed in bfloat16 or wider, within the bound.
No kernel may reach another device: no remote copies, remote signals or barrier semaphores. Data moves between devices by JAX's collectives and lax.ppermute only.
A program may use at most 128 MiB of HBM per device.

v0:
```python
import jax
import jax.numpy as jnp
from jax import lax
from jax.sharding import PartitionSpec as P

HEADS = 24
KV_HEADS = 8
HEAD_DIM = 64
EXPERTS = 32
TOPK = 8
SHIFTS = 2
CAP = 40
EPS = 1e-06
THETA = 10000.0


def from_behind(value, axis, steps):
    count = lax.axis_size(axis)
    first, last = (max(0, -steps), min(count, count - steps))
    return lax.ppermute(value, axis, [(source, source + steps) for source in range(first, last)])


def rms_norm(x, gain):
    values = x.astype(jnp.float32)
    mean_sq = jnp.mean(values * values, axis=-1, keepdims=True)
    return (values * lax.rsqrt(mean_sq + EPS) * gain).astype(jnp.bfloat16)


def rotary(x, positions):
    half = x.shape[-1] // 2
    freqs = THETA ** (-jnp.arange(half, dtype=jnp.float32) * 2.0 / x.shape[-1])
    angles = positions.astype(jnp.float32)[:, None] * freqs[None, :]
    cosine = jnp.concatenate([jnp.cos(angles), jnp.cos(angles)], axis=-1)[:, None, :]
    sine = jnp.concatenate([jnp.sin(angles), jnp.sin(angles)], axis=-1)[:, None, :]
    turned = jnp.concatenate([-x[..., half:], x[..., :half]], axis=-1)
    return x * cosine + turned * sine


def request_info(index, lengths):
    ends = jnp.cumsum(lengths, dtype=jnp.int32)
    before = ends[None, :] <= index[:, None]
    segment = jnp.sum(before.astype(jnp.int32), axis=1, dtype=jnp.int32)
    start = jnp.sum(jnp.where(before, lengths[None, :], 0), axis=1, dtype=jnp.int32)
    return (segment, index - start)


def merge_block(carry, scores, values, visible):
    best, total, acc = carry
    if visible is not None:
        scores = jnp.where(visible, scores, -1e30)
    newest = jnp.maximum(best, jnp.max(scores, axis=-1))
    probs = jnp.exp(scores - newest[..., None])
    if visible is not None:
        probs = jnp.where(visible, probs, 0.0)
    decay = jnp.exp(best - newest)
    total = total * decay + jnp.sum(probs, axis=-1)
    acc = acc * decay[..., None] + jnp.einsum(
        "tgrn,ngd->tgrd", probs.astype(jnp.bfloat16), values, preferred_element_type=jnp.float32
    )
    return (newest, total, acc)


def shards(
    tokens,
    attn_gain,
    qkv_weight,
    out_weight,
    prefix_cache,
    lengths,
    ffn_gain,
    expert_ids,
    gate_weights,
    expert_in,
    expert_out,
):
    rows = tokens.shape[1]
    model = tokens.shape[2]
    head_cols = HEADS * HEAD_DIM
    kv_cols = KV_HEADS * HEAD_DIM
    ratio = HEADS // KV_HEADS
    scale = 1.0 / HEAD_DIM**0.5
    lanes = lax.axis_size("tensor")
    prefix_len = prefix_cache.shape[1] * lanes
    own_lengths = lengths[0]
    inputs = tokens[0]
    normed = rms_norm(inputs, attn_gain)
    full_qkv, full_out = (
        lax.all_gather(qkv_weight, "dp", axis=1, tiled=True),
        lax.all_gather(out_weight, "dp", axis=0, tiled=True),
    )
    qkv = jnp.dot(normed, full_qkv, preferred_element_type=jnp.float32).astype(jnp.bfloat16)
    lane = lax.axis_index("tensor")
    q_index = lane * rows + jnp.arange(rows, dtype=jnp.int32)
    q_segment, offset = request_info(q_index, own_lengths)
    positions = prefix_len + offset
    query = rotary(
        qkv[:, :head_cols].astype(jnp.float32).reshape(rows, HEADS, HEAD_DIM), positions
    ).astype(jnp.bfloat16)
    query = query.reshape(rows, KV_HEADS, ratio, HEAD_DIM)
    keys = rotary(
        qkv[:, head_cols : head_cols + kv_cols]
        .astype(jnp.float32)
        .reshape(rows, KV_HEADS, HEAD_DIM),
        positions,
    ).astype(jnp.bfloat16)
    local_pairs = jnp.stack([keys.reshape(rows, kv_cols), qkv[:, head_cols + kv_cols :]], axis=1)
    start_carry = (
        jnp.full((rows, KV_HEADS, ratio), -1e30, jnp.float32),
        jnp.zeros((rows, KV_HEADS, ratio), jnp.float32),
        jnp.zeros((rows, KV_HEADS, ratio, HEAD_DIM), jnp.float32),
    )
    piece = lax.all_gather(prefix_cache[0], "tensor", axis=0, tiled=True)
    count = piece.shape[0]
    cached_keys = piece[:, 0].reshape(count, KV_HEADS, HEAD_DIM)
    cached_values = piece[:, 1].reshape(count, KV_HEADS, HEAD_DIM)
    scores = (
        jnp.einsum("tgrd,ngd->tgrn", query, cached_keys, preferred_element_type=jnp.float32) * scale
    )
    carry = merge_block(start_carry, scores, cached_values, None)
    window = local_pairs[None]
    for bit in range(SHIFTS):
        earlier = from_behind(window, "tensor", 2**bit)
        window = jnp.concatenate([window, earlier], axis=0)
    depth = window.shape[0]
    k_index = (
        (lane - jnp.arange(depth, dtype=jnp.int32))[:, None] * rows
        + jnp.arange(rows, dtype=jnp.int32)[None, :]
    ).reshape(-1)
    k_segment, unused = request_info(k_index, own_lengths)
    visible = (
        (k_index[None, :] >= 0)
        & (k_index[None, :] <= q_index[:, None])
        & (k_segment[None, :] == q_segment[:, None])
    )
    suffix_pairs = window.reshape(depth * rows, 2, kv_cols)
    suffix_keys = suffix_pairs[:, 0].reshape(depth * rows, KV_HEADS, HEAD_DIM)
    suffix_values = suffix_pairs[:, 1].reshape(depth * rows, KV_HEADS, HEAD_DIM)
    scores = (
        jnp.einsum("tgrd,ngd->tgrn", query, suffix_keys, preferred_element_type=jnp.float32) * scale
    )
    best, total, acc = merge_block(carry, scores, suffix_values, visible[:, None, None, :])
    attended = (acc / total[..., None]).astype(jnp.bfloat16).reshape(rows, head_cols)
    projected = jnp.dot(attended, full_out, preferred_element_type=jnp.float32)
    hidden_state = (inputs.astype(jnp.float32) + projected).astype(jnp.bfloat16)
    moe_input = rms_norm(hidden_state, ffn_gain)
    total_units = expert_in.shape[0] * lanes
    parts = total_units // EXPERTS
    unit_ff = expert_in.shape[2] // 2
    flat_ids = expert_ids[0].reshape(-1)
    onehot = (flat_ids[:, None] == jnp.arange(EXPERTS, dtype=jnp.int32)[None, :]).astype(jnp.int32)
    earlier_count = jnp.cumsum(onehot, axis=0, dtype=jnp.int32) - onehot
    slots = jnp.sum(earlier_count * onehot, axis=1, dtype=jnp.int32)
    unit_ids = flat_ids[:, None] * parts + jnp.arange(parts, dtype=jnp.int32)[None, :]
    target = (unit_ids * CAP + slots[:, None]).reshape(-1)
    row_of = jnp.repeat(jnp.arange(rows, dtype=jnp.int32), TOPK * parts)
    source = jnp.full((total_units * CAP,), rows, jnp.int32).at[target].set(row_of)
    padded_input = jnp.concatenate([moe_input, jnp.zeros((1, model), jnp.bfloat16)], axis=0)
    outgoing = padded_input[source]
    arrived = lax.all_to_all(
        outgoing.reshape(total_units, CAP, model), "tensor", split_axis=0, concat_axis=1, tiled=True
    )
    inner = jnp.einsum("erd,edf->erf", arrived, expert_in, preferred_element_type=jnp.float32)
    activated = (jax.nn.silu(inner[..., :unit_ff]) * inner[..., unit_ff:]).astype(jnp.bfloat16)
    produced = jnp.einsum(
        "erf,efd->erd", activated, expert_out, preferred_element_type=jnp.float32
    ).astype(jnp.bfloat16)
    returned = lax.all_to_all(produced, "tensor", split_axis=1, concat_axis=0, tiled=True)
    picked = returned.reshape(total_units * CAP, model)[target].reshape(rows, TOPK, parts, model)
    combined = jnp.einsum("tk,tksd->td", gate_weights[0], picked.astype(jnp.float32))
    mixed = (hidden_state.astype(jnp.float32) + combined).astype(jnp.bfloat16)
    return (hidden_state[None], mixed[None])


def solution(mesh):
    in_specs = (
        P("dp", "tensor", None),
        P(),
        P(None, "dp"),
        P("dp", None),
        P("dp", "tensor", None, None),
        P("dp", None),
        P(),
        P("dp", "tensor", None),
        P("dp", "tensor", None),
        P("tensor", None, None),
        P("tensor", None, None),
    )
    out_specs = (P("dp", "tensor", None), P("dp", "tensor", None))
    return jax.shard_map(shards, mesh=mesh, in_specs=in_specs, out_specs=out_specs, check_vma=False)
```

profile of v0, /device:TPU:1, one launch (start us, length us, event | category | flops | bytes accessed | tf_op | source)
XLA Modules:
  0.0 881.9 jit_solution(11526907995774648510)
XLA Ops:
  9.6 0.8 copy.82
  10.6 1.0 reduce-window.15
  11.9 0.8 fusion.56
  12.7 1.2 fusion.44
  14.2 9.0 %reduce-window.19 = s32[32,8,128]{2,1,0:T(8,128)S(1)} reduce-window(s32[32,8,128]{2,1,0:T(8,128)S(1)} %fusion.61, s32[]{:T(128)} %constant.24.clone.1), window={size=1x1x128 pad=0_0x0_0x127_0}, to_apply=%region_11.12 | reduce-window | flops 4161536 | bytes 262148 | tf_op jit(solution)/shard_map/reduce-window.2
  24.5 8.1 scatter_custom_fusion
  32.7 0.9 compare_and_fusion
  34.4 57.4 %all-gather.9.cloned.1.call-done = bf16[1,512,2,512]{3,2,0,1:T(2,128)(2,1)} async-done(((bf16[1,8,2,512]{3,2,0,1:T(2,128)(2,1)}), bf16[1,512,2,512]{3,2,0,1:T(2,128)(2,1)}) %all-gather.9.cloned.1.call-update) | async-done | bytes 1048592 | tf_op jit(solution)/shard_map/all_gather | solution.py:112
  91.8 4.2 fusion.70
  96.0 3.5 copy.73
  99.5 3.5 copy.74
  103.0 69.1 %all-gather.5.cloned.1.call-done = bf16[1536,2560]{1,0:T(8,128)(2,1)} async-done(((bf16[1536,640]{1,0:T(8,128)(2,1)}), bf16[1536,2560]{1,0:T(8,128)(2,1)}) %all-gather.5.cloned.1.call-update) | async-done | bytes 7864336 | tf_op jit(solution)/shard_map/all_gather | solution.py:88
  172.1 4.5 convolution_convert_fusion.1
  176.8 0.8 maximum_multiply_fusion.1
  178.5 3.9 collective-permute-start
  182.9 3.2 collective-permute-done
  186.1 1.1 pad_maximum_fusion.1
  187.2 3.7 collective-permute-start.1
  190.9 0.9 fusion.48
  191.8 4.8 bitcast_reduce_fusion
  196.6 3.7 collective-permute-done.1
  200.3 1.1 pad_maximum_fusion
  201.5 1.1 fusion.71
  202.6 1.3 copy.79
  203.8 2.1 copy.80
  205.9 1.1 fusion.2
  207.0 3.7 fusion.3
  210.7 1.5 fusion.5
  212.3 1.7 fusion.19
  215.3 1.7 fusion.37
  217.0 13.0 %all-gather.7.cloned.1.call-done = bf16[1536,1536]{1,0:T(8,128)(2,1)} async-done(((bf16[384,1536]{1,0:T(8,128)(2,1)}), bf16[1536,1536]{1,0:T(8,128)(2,1)}) %all-gather.7.cloned.1.call-update) | async-done | bytes 4718608 | tf_op jit(solution)/shard_map/all_gather | solution.py:89
  230.0 3.2 fusion.40
  233.5 9.5 %gather_fusion = bf16[2560,1536]{1,0:T(8,128)(2,1)} fusion(bf16[129,1536]{1,0:T(8,128)(2,1)S(1)} %concatenate.37, s32[3072]{0:T(1024)S(1)} %pad_clamp_fusion), kind=kCustom, calls=%fused_computation | custom fusion | bytes 15738880 | tf_op jit(solution)/shard_map/gather | solution.py:158
  243.0 185.6 %all_to_all.8 = bf16[64,40,1536]{2,1,0:T(8,128)(2,1)S(1)} all-to-all(bf16[64,40,1536]{2,1,0:T(8,128)(2,1)} %bitcast.167), channel_id=1, replica_groups=mesh['dp'=4,'tensor'=64] {'tensor'}, dimensions={0} | all-to-all | bytes 15728640 | tf_op jit(solution)/shard_map/all_to_all | solution.py:159
  428.6 4.2 convolution_bitcast_fusion
  432.8 2.3 fusion
  435.1 86.3 %copy.103 = bf16[1,2560,1536]{2,0,1:T(2,128)(2,1)} copy(bf16[1,2560,1536]{2,1,0:T(8,128)(2,1)S(1)} %fusion) | data formatting | bytes 15728640 | tf_op jit(solution)/shard_map/convert_element_type | solution.py:166
  522.0 51.5 %reduce.2 = bf16[2560,1536]{1,0:T(8,128)(2,1)} reduce(bf16[2560,1,1536]{2,1,0:T(2,128)(2,1)} %bitcast.165, bf16[]{:T(256)} %broadcast.284), dimensions={1}, to_apply=%bitcast.163.reduce_sub_computation | reduce | bytes 15728642
  573.5 17.7 %reshape.394 = bf16[64,2,30720]{2,1,0:T(2,128)(2,1)} reshape(bf16[2560,1536]{1,0:T(8,128)(2,1)} %reduce.2) | data formatting | bytes 15728640
  591.1 6.4 all-to-all-start.1
  597.8 174.3 %all-to-all-done.1 = bf16[64,2,30720]{2,1,0:T(2,128)(2,1)} async-done(((bf16[64,2,30720]{2,1,0:T(2,128)(2,1)}), bf16[64,2,30720]{2,1,0:T(2,128)(2,1)}, u32[]{:S(2)}, u32[]{:S(2)}) %all-to-all-start.1) | async-done | bytes 7864352 | tf_op jit(solution)/shard_map/all_to_all | solution.py:167
  772.1 38.0 %reshape.395 = bf16[2560,1,1536]{2,1,0:T(2,128)(2,1)} reshape(bf16[64,2,30720]{2,1,0:T(2,128)(2,1)} %all-to-all-done.1) | data formatting | bytes 15728640
  810.1 10.8 %copy.102 = bf16[1,2560,1536]{2,1,0:T(8,128)(2,1)} copy(bf16[1,2560,1536]{2,0,1:T(2,128)(2,1)} %bitcast.166) | data formatting | bytes 15728640
  820.9 17.5 %gather_fusion.1 = bf16[2048,1536]{1,0:T(8,128)(2,1)} fusion(bf16[2560,1536]{1,0:T(8,128)(2,1)} %bitcast.164, s32[2048]{0:T(1024)S(1)} %broadcast_clamp_fusion), kind=kCustom, calls=%fused_computation.1 | custom fusion | bytes 12591104 | tf_op jit(solution)/shard_map/gather | solution.py:168
  838.4 14.1 %reshape.358 = f32[128,8,2,1536]{3,2,1,0:T(2,128)} reshape(bf16[2048,1536]{1,0:T(8,128)(2,1)} %gather_fusion.1) | data formatting | bytes 18874368 | tf_op jit(solution)/shard_map/convert_element_type | solution.py:169
  852.6 18.9 %reduce_sum.89 = bf16[128,8,1536]{2,1,0:T(8,128)(2,1)} reduce(f32[128,8,2,1536]{3,2,1,0:T(2,128)} %reshape.358, f32[]{:T(128)} %constant.19.clone.1), dimensions={2}, to_apply=%region_15.16 | reduce | flops 1572864 | bytes 15728644 | tf_op jit(solution)/shard_map/tk,tksd->td/reduce_sum | solution.py:169
  871.4 2.8 fusion.72
  874.3 0.8 fusion.51
  (91 shorter events, 9.0 us)
Async XLA Ops:
  7.2 421.4 %copy-start = (bf16[1,1536,512]{2,1,0:T(8,128)(2,1)S(1)}, bf16[1,1536,512]{2,1,0:T(8,128)(2,1)}, u32[]{:S(2)}) copy-start(bf16[1,1536,512]{2,1,0:T(8,128)(2,1)} %param.20) | copy-start | bytes 4718596
  7.2 84.6 %all-gather.9.cloned.1.call-start = ((), (), s32[]{:S(2)}) async-start(), calls=%async_computation.4 | async-start | bytes 1064960 | tf_op jit(solution)/shard_map/all_gather | solution.py:112
  7.9 164.2 %all-gather.5.cloned.1.call-start = ((), (), s32[]{:S(2)}) async-start(), calls=%async_computation.2 | async-start | bytes 9830400 | tf_op jit(solution)/shard_map/all_gather | solution.py:88
  8.7 163.5 %copy-start.2 = (bf16[1,128,1536]{2,1,0:T(8,128)(2,1)S(1)}, bf16[1,128,1536]{2,1,0:T(8,128)(2,1)}, u32[]{:S(2)}) copy-start(bf16[1,128,1536]{2,1,0:T(8,128)(2,1)} %param.11) | copy-start | bytes 1179652
  8.7 163.4 %copy-start.8 = (f32[1536]{0:T(1024)S(1)}, f32[1536]{0:T(1024)}, u32[]{:S(2)}) copy-start(f32[1536]{0:T(1024)} %param.12) | copy-start | bytes 18436
  8.7 221.3 %all-gather.7.cloned.1.call-start = ((), (), s32[]{:S(2)}) async-start(), calls=%async_computation.3 | async-start | bytes 5898240 | tf_op jit(solution)/shard_map/all_gather | solution.py:89
  24.4 8.2 copy-start.9
  34.2 68.8 %copy-start.7 = (f32[128,64]{0,1:T(8,128)}, f32[128,64]{0,1:T(8,128)S(1)}, u32[]{:S(2)}) copy-start(f32[128,64]{0,1:T(8,128)S(1)} %get-tuple-element.27) | copy-start | bytes 98308
  178.5 7.5 collective-permute-start
  187.2 13.1 %collective-permute-start.1 = (bf16[2,128,2,512]{3,1,2,0:T(8,128)(2,1)S(1)}, bf16[2,128,2,512]{3,1,2,0:T(8,128)(2,1)S(1)}, u32[]{:S(2)}, u32[]{:S(2)}) collective-permute-start(bf16[2,128,2,512]{3,1,2,0:T(8,128)(2,1)S(1)} %pad_maximum_fusion.1), channel_id=1, source_target_pairs={{0,2},{1,3},{2,4},{3,5},{4,6},{5,7},{6,8},{7,9},{8,10},{9,11},{10,... | collective-permute-start | bytes 1572872 | tf_op jit(solution)/shard_map/ppermute | solution.py:20
  191.8 14.1 %copy-start.4 = (pred[128,512]{0,1:T(8,128)(4,1)S(1)}, pred[128,512]{0,1:T(8,128)(4,1)}, u32[]{:S(2)}) copy-start(pred[128,512]{0,1:T(8,128)(4,1)} %compare_and_fusion) | copy-start | bytes 196612
  207.0 5.3 copy-start.6
  212.2 2.4 slice-start
  212.3 2.4 copy-start.5
  212.3 3.0 slice-start.1
  215.3 18.0 %copy-start.11 = (f32[1536]{0:T(1024)S(1)}, f32[1536]{0:T(1024)}, u32[]{:S(2)}) copy-start(f32[1536]{0:T(1024)} %param.17) | copy-start | bytes 18436
  233.2 641.1 %copy-start.3 = (bf16[128,1536]{1,0:T(8,128)(2,1)}, bf16[128,1536]{1,0:T(8,128)(2,1)S(1)}, u32[]{:S(2)}) copy-start(bf16[128,1536]{1,0:T(8,128)(2,1)S(1)} %get-tuple-element.26) | copy-start | bytes 1179652
  428.6 4.3 copy-start.13
  591.1 6.4 copy-start.12
  591.1 6.6 copy-start.10
  591.1 181.0 %all-to-all-start.1 = ((bf16[64,2,30720]{2,1,0:T(2,128)(2,1)}), bf16[64,2,30720]{2,1,0:T(2,128)(2,1)}, u32[]{:S(2)}, u32[]{:S(2)}) async-start(bf16[64,2,30720]{2,1,0:T(2,128)(2,1)} %reshape.394), calls=%async_computation.1 | async-start | bytes 15728640 | tf_op jit(solution)/shard_map/all_to_all | solution.py:167
  852.6 22.6 %copy-start.1 = (bf16[1,1536,512]{2,1,0:T(8,128)(2,1)S(1)}, bf16[1,1536,512]{2,1,0:T(8,128)(2,1)}, u32[]{:S(2)}) copy-start(bf16[1,1536,512]{2,1,0:T(8,128)(2,1)} %param.20) | copy-start | bytes 4718596
Sparse Core Ops, SparseCore 0:
  10.8 80.9 all-gather.8
  93.6 78.4 all-gather.4
  173.9 56.0 all-gather.6
where the time goes:
time: 890 us; the launch traced here: 882 us
  waiting for transfers between devices  323 us (36%)
  local copies, waits for them, and re-layouts  222 us (25%)
  blocking collectives  186 us (21%)
  other arithmetic  96.3 us (11%)
  matrix products  26.4 us (3%)
  between operations  14.5 us (2%)
  starting transfers between devices  14.1 us (2%)
    all_to_all x1, blocking collectives, shards(): lax.all_to_all(outgoing.reshape(total_units, CAP, model), 'tensor', split...  186 us
    all_to_all x1, waiting for transfers between devices, shards(): lax.all_to_all(produced, 'tensor', split_axis=1, concat_axis=0, tiled=True)  174 us
    convert_element_type x1, local copies, waits for them, and re-layouts, shards(): produced = jnp.einsum('erf,efd->erd', activated, expert_out, preferred_el...  86.3 us
    all_gather x1, waiting for transfers between devices, shards(): lax.all_gather(qkv_weight, 'dp', axis=1, tiled=True)  69.1 us
    unnamed x37, local copies, waits for them, and re-layouts  69.1 us
    all_gather x1, waiting for transfers between devices, shards(): piece = lax.all_gather(prefix_cache[0], 'tensor', axis=0, tiled=True)  57.4 us
    unnamed x2, other arithmetic  51.5 us
    reduce_sum x1, other arithmetic, shards(): jnp.einsum('tk,tksd->td', gate_weights[0], picked.astype(jnp.float32))  18.9 us
  transfers between devices with their start and end apart: 6, of which 6 were waited for; matrix products, arithmetic and copies ran while one was open for 7% of the time, Pallas kernels for 0%

commit v1 on v0

--- a/solution.py
+++ b/solution.py
@@ -12,6 +12,9 @@
 CAP = 40
 EPS = 1e-06
 THETA = 10000.0
+divide_samples_all_for = lambda axis_id, pos_dim, local_block: jnp.concatenate(
+    lax.all_to_all(jnp.stack([local_block] * lax.axis_size(axis_id)), axis_id, 0, 0), pos_dim
+)
 
 
 def from_behind(value, axis, steps):
@@ -109,7 +112,7 @@
         jnp.zeros((rows, KV_HEADS, ratio), jnp.float32),
         jnp.zeros((rows, KV_HEADS, ratio, HEAD_DIM), jnp.float32),
     )
-    piece = lax.all_gather(prefix_cache[0], "tensor", axis=0, tiled=True)
+    piece = divide_samples_all_for("tensor", 0, prefix_cache[0])
     count = piece.shape[0]
     cached_keys = piece[:, 0].reshape(count, KV_HEADS, HEAD_DIM)
     cached_values = piece[:, 1].reshape(count, KV_HEADS, HEAD_DIM)

time: 890 us -> 813 us (0.913)
  waiting for transfers between devices: 323 us -> 240 us
  starting transfers between devices: 14.1 us -> 27.1 us
    all_gather x1 -> x0, waiting for transfers between devices: 57.4 us -> none  [shards(): piece = lax.all_gather(prefix_cache[0], 'tensor', axis=0, tiled=True)]
    all_gather x1, waiting for transfers between devices: 69.1 us -> 40.1 us  [shards(): lax.all_gather(qkv_weight, 'dp', axis=1, tiled=True)]
    all_to_all x0 -> x1, starting transfers between devices: none -> 13.2 us  [lax.all_to_all(jnp.stack([local_block] * lax.axis_size(axis_id)), axis_id...]
    unnamed x37 -> x39, local copies, waits for them, and re-layouts: 69.1 us -> 69 us
where the time goes in v1:
time: 813 us; the launch traced here: 805 us
  waiting for transfers between devices  240 us (30%)
  local copies, waits for them, and re-layouts  216 us (27%)
  blocking collectives  186 us (23%)
  other arithmetic  94.6 us (12%)
  starting transfers between devices  27.1 us (3%)
  matrix products  26.3 us (3%)
  between operations  14.8 us (2%)
    all_to_all x1, blocking collectives, shards(): lax.all_to_all(outgoing.reshape(total_units, CAP, model), 'tensor', split...  186 us
    all_to_all x1, waiting for transfers between devices, shards(): lax.all_to_all(produced, 'tensor', split_axis=1, concat_axis=0, tiled=True)  174 us
    convert_element_type x1, local copies, waits for them, and re-layouts, shards(): produced = jnp.einsum('erf,efd->erd', activated, expert_out, preferred_el...  86.3 us
    unnamed x39, local copies, waits for them, and re-layouts  69 us
    unnamed x2, other arithmetic  51.5 us
    all_gather x1, waiting for transfers between devices, shards(): lax.all_gather(qkv_weight, 'dp', axis=1, tiled=True)  40.1 us
    reduce_sum x1, other arithmetic, shards(): jnp.einsum('tk,tksd->td', gate_weights[0], picked.astype(jnp.float32))  18.9 us
    gather x1, local copies, waits for them, and re-layouts, shards(): returned.reshape(total_units * CAP, model)[target]  17.6 us
  transfers between devices with their start and end apart: 6, of which 6 were waited for; matrix products, arithmetic and copies ran while one was open for 7% of the time, Pallas kernels for 0%

profile of v1, /device:TPU:1, one launch (start us, length us, event | category | flops | bytes accessed | tf_op | source)
XLA Modules:
  0.0 804.9 jit_solution(8139650020458573634)
XLA Ops:
  7.9 0.7 copy.74
  8.7 1.1 stack.9
  9.8 13.2 %all-to-all-start = ((bf16[64,8,2,512]{3,1,2,0:T(8,128)(2,1)}), bf16[64,8,2,512]{3,1,2,0:T(8,128)(2,1)}, u32[]{:S(2)}, u32[]{:S(2)}) async-start(bf16[64,8,2,512]{3,1,2,0:T(8,128)(2,1)} %stack.9), calls=%async_computation | async-start | bytes 2097152 | tf_op jit(solution)/shard_map/all_to_all | solution.py:16
  24.9 9.0 %reduce-window.19 = s32[32,8,128]{2,1,0:T(8,128)S(1)} reduce-window(s32[32,8,128]{2,1,0:T(8,128)S(1)} %fusion.61, s32[]{:T(128)} %constant.24.clone.1), window={size=1x1x128 pad=0_0x0_0x127_0}, to_apply=%region_11.12 | reduce-window | flops 4161536 | bytes 262148 | tf_op jit(solution)/shard_map/reduce-window.2
  36.7 8.1 %scatter_custom_fusion = s32[2560]{0:T(1024)S(1)} fusion(s32[2048]{0:T(1024)S(1)} %bitcast.189, s32[2048]{0:T(1024)S(1)} %reshape.384, s32[]{:T(128)} %constant.23.clone.1), kind=kCustom, calls=%fused_computation.94 | custom fusion | bytes 10244 | tf_op jit(solution)/shard_map/scatter | solution.py:159
  45.9 0.9 compare_and_fusion
  46.8 4.6 all-to-all-done
  51.4 1.3 copy.107
  52.8 1.1 copy.76
  53.8 1.0 copy.77
  54.9 40.1 %all-gather.3.cloned.1.call-done = bf16[1536,2560]{1,0:T(8,128)(2,1)} async-done(((bf16[1536,640]{1,0:T(8,128)(2,1)}), bf16[1536,2560]{1,0:T(8,128)(2,1)}) %all-gather.3.cloned.1.call-update) | async-done | bytes 7864336 | tf_op jit(solution)/shard_map/all_gather | solution.py:91
  94.9 4.5 convolution_convert_fusion.1
  99.6 0.8 maximum_multiply_fusion.1
  100.6 0.7 maximum_bitcast_fusion
  101.3 3.8 collective-permute-start
  105.6 3.2 collective-permute-done
  108.8 1.1 pad_maximum_fusion.1
  109.9 3.7 collective-permute-start.1
  113.6 0.9 fusion.48
  114.5 4.8 bitcast_reduce_fusion
  119.3 3.8 collective-permute-done.1
  123.0 1.1 pad_maximum_fusion
  124.3 1.1 fusion.71
  125.3 1.3 copy.82
  126.6 2.1 copy.83
  128.7 1.1 fusion.2
  129.8 3.7 fusion.3
  133.5 1.5 fusion.5
  135.1 1.7 fusion.19
  138.1 1.7 fusion.37
  139.8 12.9 %all-gather.5.cloned.1.call-done = bf16[1536,1536]{1,0:T(8,128)(2,1)} async-done(((bf16[384,1536]{1,0:T(8,128)(2,1)}), bf16[1536,1536]{1,0:T(8,128)(2,1)}) %all-gather.5.cloned.1.call-update) | async-done | bytes 4718608 | tf_op jit(solution)/shard_map/all_gather | solution.py:92
  152.7 3.2 fusion.40
  156.2 9.5 %gather_fusion = bf16[2560,1536]{1,0:T(8,128)(2,1)} fusion(bf16[129,1536]{1,0:T(8,128)(2,1)S(1)} %concatenate.37, s32[3072]{0:T(1024)S(1)} %copy-done.9), kind=kCustom, calls=%fused_computation | custom fusion | bytes 15738880 | tf_op jit(solution)/shard_map/gather | solution.py:161
  165.7 185.6 %all_to_all.23 = bf16[64,40,1536]{2,1,0:T(8,128)(2,1)S(1)} all-to-all(bf16[64,40,1536]{2,1,0:T(8,128)(2,1)} %bitcast.169), channel_id=1, replica_groups=mesh['dp'=4,'tensor'=64] {'tensor'}, dimensions={0} | all-to-all | bytes 15728640 | tf_op jit(solution)/shard_map/all_to_all | solution.py:162
  351.2 4.2 convolution_bitcast_fusion
  355.5 2.3 fusion
  357.8 86.3 %copy.108 = bf16[1,2560,1536]{2,0,1:T(2,128)(2,1)} copy(bf16[1,2560,1536]{2,1,0:T(8,128)(2,1)S(1)} %fusion) | data formatting | bytes 15728640 | tf_op jit(solution)/shard_map/convert_element_type | solution.py:169
  444.7 51.5 %reduce.2 = bf16[2560,1536]{1,0:T(8,128)(2,1)} reduce(bf16[2560,1,1536]{2,1,0:T(2,128)(2,1)} %bitcast.167, bf16[]{:T(256)} %broadcast.285), dimensions={1}, to_apply=%bitcast.165.reduce_sub_computation | reduce | bytes 15728642
  496.2 17.6 %reshape.398 = bf16[64,2,30720]{2,1,0:T(2,128)(2,1)} reshape(bf16[2560,1536]{1,0:T(8,128)(2,1)} %reduce.2) | data formatting | bytes 15728640
  513.8 6.4 all-to-all-start.2
  520.4 174.4 %all-to-all-done.2 = bf16[64,2,30720]{2,1,0:T(2,128)(2,1)} async-done(((bf16[64,2,30720]{2,1,0:T(2,128)(2,1)}), bf16[64,2,30720]{2,1,0:T(2,128)(2,1)}, u32[]{:S(2)}, u32[]{:S(2)}) %all-to-all-start.2) | async-done | bytes 7864352 | tf_op jit(solution)/shard_map/all_to_all | solution.py:170
  694.8 38.0 %reshape.399 = bf16[2560,1,1536]{2,1,0:T(2,128)(2,1)} reshape(bf16[64,2,30720]{2,1,0:T(2,128)(2,1)} %all-to-all-done.2) | data formatting | bytes 15728640
  732.7 10.8 %copy.106 = bf16[1,2560,1536]{2,1,0:T(8,128)(2,1)} copy(bf16[1,2560,1536]{2,0,1:T(2,128)(2,1)} %bitcast.168) | data formatting | bytes 15728640
  743.6 17.6 %gather_fusion.1 = bf16[2048,1536]{1,0:T(8,128)(2,1)} fusion(bf16[2560,1536]{1,0:T(8,128)(2,1)} %bitcast.166, s32[2048]{0:T(1024)S(1)} %broadcast_clamp_fusion), kind=kCustom, calls=%fused_computation.1 | custom fusion | bytes 12591104 | tf_op jit(solution)/shard_map/gather | solution.py:171
  761.1 14.1 %reshape.363 = f32[128,8,2,1536]{3,2,1,0:T(2,128)} reshape(bf16[2048,1536]{1,0:T(8,128)(2,1)} %gather_fusion.1) | data formatting | bytes 18874368 | tf_op jit(solution)/shard_map/convert_element_type | solution.py:172
  775.3 18.9 %reduce_sum.89 = bf16[128,8,1536]{2,1,0:T(8,128)(2,1)} reduce(f32[128,8,2,1536]{3,2,1,0:T(2,128)} %reshape.363, f32[]{:T(128)} %constant.19.clone.1), dimensions={2}, to_apply=%region_15.16 | reduce | flops 1572864 | bytes 15728644 | tf_op jit(solution)/shard_map/tk,tksd->td/reduce_sum | solution.py:172
  794.1 2.8 fusion.72
  797.0 0.8 fusion.51
  (95 shorter events, 9.5 us)
Async XLA Ops:
  7.2 344.1 %copy-start = (bf16[1,1536,512]{2,1,0:T(8,128)(2,1)S(1)}, bf16[1,1536,512]{2,1,0:T(8,128)(2,1)}, u32[]{:S(2)}) copy-start(bf16[1,1536,512]{2,1,0:T(8,128)(2,1)} %param.20) | copy-start | bytes 4718596
  7.2 16.5 %copy-start.11 = (s32[1,128,8]{1,2,0:T(8,128)S(1)}, s32[1,128,8]{1,2,0:T(8,128)}, u32[]{:S(2)}) copy-start(s32[1,128,8]{1,2,0:T(8,128)} %param.18) | copy-start | bytes 12292
  7.2 16.8 %copy-start.13 = (s32[1,256]{1,0:T(1,128)S(1)}, s32[1,256]{1,0:T(1,128)}, u32[]{:S(2)}) copy-start(s32[1,256]{1,0:T(1,128)} %param.16) | copy-start | bytes 3076
  7.2 37.8 %copy-start.2 = (bf16[1,128,1536]{2,1,0:T(8,128)(2,1)S(1)}, bf16[1,128,1536]{2,1,0:T(8,128)(2,1)}, u32[]{:S(2)}) copy-start(bf16[1,128,1536]{2,1,0:T(8,128)(2,1)} %param.11) | copy-start | bytes 1179652
  7.2 87.7 %all-gather.3.cloned.1.call-start = ((), (), s32[]{:S(2)}) async-start(), calls=%async_computation.3 | async-start | bytes 9830400 | tf_op jit(solution)/shard_map/all_gather | solution.py:91
  9.8 41.6 %all-to-all-start = ((bf16[64,8,2,512]{3,1,2,0:T(8,128)(2,1)}), bf16[64,8,2,512]{3,1,2,0:T(8,128)(2,1)}, u32[]{:S(2)}, u32[]{:S(2)}) async-start(bf16[64,8,2,512]{3,1,2,0:T(8,128)(2,1)} %stack.9), calls=%async_computation | async-start | bytes 2097152 | tf_op jit(solution)/shard_map/all_to_all | solution.py:16
  22.9 72.0 %copy-start.8 = (f32[1536]{0:T(1024)S(1)}, f32[1536]{0:T(1024)}, u32[]{:S(2)}) copy-start(f32[1536]{0:T(1024)} %param.12) | copy-start | bytes 18436
  23.0 129.7 %all-gather.5.cloned.1.call-start = ((), (), s32[]{:S(2)}) async-start(), calls=%async_computation.4 | async-start | bytes 5898240 | tf_op jit(solution)/shard_map/all_gather | solution.py:92
  35.5 0.6 copy-start.7
  101.3 7.4 collective-permute-start
  109.9 13.1 %collective-permute-start.1 = (bf16[2,128,2,512]{3,1,2,0:T(8,128)(2,1)S(1)}, bf16[2,128,2,512]{3,1,2,0:T(8,128)(2,1)S(1)}, u32[]{:S(2)}, u32[]{:S(2)}) collective-permute-start(bf16[2,128,2,512]{3,1,2,0:T(8,128)(2,1)S(1)} %pad_maximum_fusion.1), channel_id=1, source_target_pairs={{0,2},{1,3},{2,4},{3,5},{4,6},{5,7},{6,8},{7,9},{8,10},{9,11},{10,... | collective-permute-start | bytes 1572872 | tf_op jit(solution)/shard_map/ppermute | solution.py:23
  114.5 14.2 %copy-start.4 = (pred[128,512]{0,1:T(8,128)(4,1)S(1)}, pred[128,512]{0,1:T(8,128)(4,1)}, u32[]{:S(2)}) copy-start(pred[128,512]{0,1:T(8,128)(4,1)} %compare_and_fusion) | copy-start | bytes 196612
  129.8 5.3 copy-start.6
  135.0 2.4 slice-start
  135.0 2.4 copy-start.5
  135.1 3.0 slice-start.1
  138.1 17.9 %copy-start.10 = (f32[1536]{0:T(1024)S(1)}, f32[1536]{0:T(1024)}, u32[]{:S(2)}) copy-start(f32[1536]{0:T(1024)} %param.17) | copy-start | bytes 18436
  138.1 18.1 %copy-start.9 = (s32[3072]{0:T(1024)S(1)}, s32[3072]{0:T(1024)}, u32[]{:S(2)}) copy-start(s32[3072]{0:T(1024)} %pad_clamp_fusion) | copy-start | bytes 36868
  155.9 641.1 %copy-start.3 = (bf16[128,1536]{1,0:T(8,128)(2,1)}, bf16[128,1536]{1,0:T(8,128)(2,1)S(1)}, u32[]{:S(2)}) copy-start(bf16[128,1536]{1,0:T(8,128)(2,1)S(1)} %get-tuple-element.26) | copy-start | bytes 1179652
  351.2 4.3 copy-start.14
  513.8 6.4 copy-start.12
  513.8 180.9 %all-to-all-start.2 = ((bf16[64,2,30720]{2,1,0:T(2,128)(2,1)}), bf16[64,2,30720]{2,1,0:T(2,128)(2,1)}, u32[]{:S(2)}, u32[]{:S(2)}) async-start(bf16[64,2,30720]{2,1,0:T(2,128)(2,1)} %reshape.398), calls=%async_computation.2 | async-start | bytes 15728640 | tf_op jit(solution)/shard_map/all_to_all | solution.py:170
  775.3 22.6 %copy-start.1 = (bf16[1,1536,512]{2,1,0:T(8,128)(2,1)S(1)}, bf16[1,1536,512]{2,1,0:T(8,128)(2,1)}, u32[]{:S(2)}) copy-start(bf16[1,1536,512]{2,1,0:T(8,128)(2,1)} %param.20) | copy-start | bytes 4718596
Sparse Core Ops, SparseCore 0:
  9.9 85.0 all-gather.2
  96.7 55.8 all-gather.4
